TPU v7x, 512 devices: a whole 4x4x16 slice. The times are simulated.
512 devices in a mesh: plane: 16 (over x, z_hi), tile: 32 (over z_lo, y, core).
Axes of the slice: x: 4, y: 4, z: 16 (z_hi: 4, z_lo: 4; z = z_hi * 4 + z_lo), core: 2. Of those that a mesh axis runs over, the one named last changes fastest.
Arguments:
- density: float32 [48, 256, 2048], P('plane', 'tile'), may hold values from -6 to 6
- plane_slot: int32 [48], replicated, may hold values from 0 to 95, as said below
- paint_weight: float32 [32, 9], replicated, may hold values from -2 to 2
- paint_bias: float32 [32], replicated, may hold values from -0.5 to 0.5
- mix_weight: float32 [32], replicated, may hold values from -1 to 1
- short_kernel: float32 [5, 5], replicated, may hold values from -1 to 1
Outputs:
- distortion: float32 [4, 48, 256, 2048], P(None, 'plane', 'tile')
Inputs may be any that keep to these rules, and one draw needn't show every extreme that they name: `plane_slot`: strictly increasing along the planes; the first is 0 and the last is 95.
All inputs are finite; a program needn't handle non-finite values.
Results may differ from a plain program's by a relative error of at most 0.00026.
Values sent between devices are 32-bit elements; how exact they have to be, the bound alone decides.
No kernel may reach another device: no remote copies, remote signals or barrier semaphores. Data moves between devices by JAX's collectives and lax.ppermute only.
A program may use at most 64 MiB of HBM per device.

v0:
```python
import math
import jax
import jax.numpy as jnp
from jax import lax
from jax.sharding import PartitionSpec as P

highest = lax.Precision.HIGHEST
lens_gain = 0.25


def extended_2(block, sides, width):
    for axis, dim in sides:
        count = lax.axis_size(axis)
        forward = [(i, i + 1) for i in range(count - 1)]
        backward = [(target, source) for source, target in forward]
        low = lax.ppermute(
            lax.slice_in_dim(block, block.shape[dim] - width, None, axis=dim), axis, forward
        )
        high = lax.ppermute(lax.slice_in_dim(block, 0, width, axis=dim), axis, backward)
        block = jnp.concatenate([low, block, high], axis=dim)
    return block


def from_behind(value, axis, by):
    devices = lax.axis_size(axis)
    pairs = [(i, i + by) for i in range(devices) if 0 <= i + by < devices]
    return lax.ppermute(value, axis, pairs)


def paint_rows(extended, paint_weight, paint_bias, mix_weight):
    row_count = extended.shape[-2] - 4
    col_count = extended.shape[-1]
    padded = jnp.pad(extended, [(0, 0)] * (extended.ndim - 1) + [(2, 2)])
    stacked = jnp.stack(
        [
            padded[
                ...,
                2 + 2 * row_step : 2 + 2 * row_step + row_count,
                2 + 2 * col_step : 2 + 2 * col_step + col_count,
            ]
            for row_step in (-1, 0, 1)
            for col_step in (-1, 0, 1)
        ],
        axis=0,
    )
    before = jnp.einsum("ct,t...->c...", paint_weight, stacked, precision=highest)
    hidden = jnp.tanh(before + paint_bias.reshape((-1,) + (1,) * (before.ndim - 1)))
    return jnp.einsum("c,c...->...", mix_weight, hidden, precision=highest)


def short_rows(extended, short_kernel):
    row_count = extended.shape[-2] - 4
    col_count = extended.shape[-1]
    padded = jnp.pad(extended, [(0, 0)] * (extended.ndim - 1) + [(2, 2)])
    running = jnp.zeros(extended.shape[:-2] + (row_count, col_count), jnp.float32)
    for row_tap in range(5):
        for col_tap in range(5):
            running = (
                running
                + short_kernel[row_tap, col_tap]
                * padded[..., row_tap : row_tap + row_count, col_tap : col_tap + col_count]
            )
    return running


def hessian_rows(extended):
    padded = jnp.pad(extended, [(0, 0)] * (extended.ndim - 1) + [(1, 1)])
    center = padded[..., 1:-1, 1:-1]
    second_rows = padded[..., 2:, 1:-1] - 2.0 * center + padded[..., :-2, 1:-1]
    second_cols = padded[..., 1:-1, 2:] - 2.0 * center + padded[..., 1:-1, :-2]
    mixed_part = (
        padded[..., 2:, 2:] - padded[..., 2:, :-2] - padded[..., :-2, 2:] + padded[..., :-2, :-2]
    ) * 0.25
    return jnp.stack([second_rows, second_cols, mixed_part], axis=0)


def lens_step(lens_state, shear_field, mixing, bending):
    previous = lens_state[0:2]
    current = lens_state[2:4]
    bent_first = shear_field[0] * current[0] + shear_field[2] * current[1]
    bent_second = shear_field[2] * current[0] + shear_field[1] * current[1]
    bent_rows = jnp.stack([bent_first, bent_second], axis=0)
    advanced = (1.0 - mixing) * previous + mixing * current - bending * bent_rows
    return jnp.concatenate([current, advanced], axis=0)


def distances(plane_slot, slot_total):
    distance = (plane_slot.astype(jnp.float32) + 1.0) / slot_total
    before = jnp.concatenate([jnp.zeros((1,), jnp.float32), distance[:-1]])
    after = jnp.concatenate(
        [distance[1:], jnp.full((1,), (slot_total + 1.0) / slot_total, jnp.float32)]
    )
    mixing = before * (after - distance) / (distance * (after - before))
    bending = lens_gain * (after - distance) / after
    return (mixing, bending)


def coarse_kernel(row_global, col_global, scale):
    gap = row_global.astype(jnp.float32)[:, None] - col_global.astype(jnp.float32)[None, :]
    return jnp.exp(-jnp.abs(gap) / scale)


def start_for(row_count, col_count):
    pattern = jnp.array([[1.0, 0.0], [0.0, 1.0], [1.0, 0.0], [0.0, 1.0]], jnp.float32)
    return jnp.broadcast_to(pattern[:, :, None, None], (4, 2, row_count, col_count))


def body(density, plane_slot, paint_weight, paint_bias, mix_weight, short_kernel):
    plane_count, row_count, col_count = density.shape
    tile_count = lax.axis_size("tile")
    tile_index = lax.axis_index("tile")
    plane_index = lax.axis_index("plane")
    total_rows = row_count * tile_count
    coarse_here = row_count // 4
    coarse_cols = col_count // 4
    row_scale = total_rows / 16.0
    col_scale = col_count / 16.0
    long_gain = 1.0 / math.sqrt(row_scale * col_scale)
    col_kernel = coarse_kernel(
        jnp.arange(coarse_cols, dtype=jnp.int32),
        jnp.arange(coarse_cols, dtype=jnp.int32),
        col_scale,
    )
    mixing_all, bending_all = distances(plane_slot, 2 * plane_slot.shape[0])
    mixing_here = lax.dynamic_slice_in_dim(mixing_all, plane_index * plane_count, plane_count)
    bending_here = lax.dynamic_slice_in_dim(bending_all, plane_index * plane_count, plane_count)
    extended = extended_2(density, (("tile", 1),), 2)
    convergence = paint_rows(extended, paint_weight, paint_bias, mix_weight)
    convergence_wide = extended_2(convergence, (("tile", 1),), 2)
    short_part = short_rows(convergence_wide, short_kernel)
    row_global = tile_index * coarse_here + 0 + jnp.arange(coarse_here, dtype=jnp.int32)
    coarse = convergence.reshape(plane_count, coarse_here, 4, coarse_cols, 4).mean(axis=(2, 4))
    received = lax.all_gather(coarse, "tile", axis=1, tiled=True)
    span_cols = received.shape[1]
    kernel_block = coarse_kernel(row_global, jnp.arange(span_cols, dtype=jnp.int32), row_scale)
    summed = jnp.einsum("ik,pkx->pix", kernel_block, received, precision=highest)
    potential = short_part + jnp.repeat(
        jnp.repeat(
            long_gain * jnp.einsum("pix,xy->piy", summed, col_kernel, precision=highest), 4, axis=1
        ),
        4,
        axis=2,
    )
    potential_wide = extended_2(potential, (("tile", 1),), 1)
    shear_field = hessian_rows(potential_wide)

    def run_planes(lens_state):
        results = []
        for plane_pos in range(plane_count):
            lens_state = lens_step(
                lens_state,
                shear_field[:, plane_pos],
                mixing_here[plane_pos],
                bending_here[plane_pos],
            )
            results.append(lens_state[2:4].reshape(4, row_count, col_count))
        return (lens_state, jnp.stack(results, axis=1))

    start_state = start_for(row_count, col_count)

    def relay_turn(iteration, state_in):
        state_out, unused_results = run_planes(state_in)
        incoming = from_behind(state_out, "plane", 1)
        return jnp.where(plane_index == 0, start_state, incoming)

    state_in = lax.fori_loop(0, lax.axis_size("plane") - 1, relay_turn, start_state)
    unused_state, results = run_planes(state_in)
    return results


def solution(mesh):
    placed = (P("plane", "tile", None), P(), P(), P(), P(), P())
    return jax.shard_map(
        body, mesh=mesh, in_specs=placed, out_specs=P(None, "plane", "tile", None), check_vma=False
    )
```

profile of v0, /device:TPU:108, one launch (start us, length us, event | category | flops | bytes accessed | tf_op | source)
XLA Modules:
  0.0 1031.1 jit_solution(7631755121506922006)
XLA Ops:
  24.1 6.6 stack.90
  30.8 7.6 fusion.61
  43.0 7.9 reshape.65
  59.8 36.7 %all_gather.3 = f32[3,64,512]{2,0,1:T(4,128)S(1)} all-gather(f32[3,2,512]{2,0,1:T(4,128)S(1)} %copy.220), channel_id=1, replica_groups=mesh['plane'=16,'tile'=32] {'tile'}, dimensions={1}, use_global_device_ids=true | all-gather | bytes 405504 | tf_op jit(solution)/shard_map/all_gather | solution.py:133
  102.8 17.4 %fusion.33 = f32[3,8,2048]{2,1,0:T(8,128)S(1)} fusion(f32[3,8,2048]{2,1,0:T(8,128)S(1)} %copy.225, f32[3,8,2048]{2,1,0:T(8,128)S(1)} %bitcast.137, f32[3,2,2048]{2,1,0:T(2,128)} %collective-permute-done.4, f32[3,2,2048]{2,1,0:T(2,128)} %collective-permute-done.3, f32[3,12,2052]{2,1,0:T(8,128)S(1)} %select_maximum_fusion.2, f32[]{:T(128)} %bitcast.37, ...), kind=kLoop, calls=%fused_computation.74 | loop fusion | flops 2654208 | bytes 4620388 | tf_op jit(solution)/shard_map/add | solution.py:137
  128.2 895.2 %while.13 = (s32[]{:T(128)}, f32[4,2,8,2048]{3,2,1,0:T(8,128)S(1)}, pred[]{:T(512)}, f32[]{:T(128)}, f32[3]{0:T(128)S(1)}, /*index=5*/f32[]{:T(128)}, f32[3]{0:T...) while((s32[]{:T(128)}, f32[4,2,8,2048]{3,2,1,0:T(8,128)S(1)}, ...), condition=%wide.region_2.3_spmd.clone, body=%wide.region_1.2_spmd.sunk.clone.sunk | while | flops 2818050 | bytes 11469090 | solution.py:166
  135.6 9.1 collective-permute-start
  144.7 35.9 %collective-permute-done = f32[4,2,8,2048]{3,2,1,0:T(8,128)S(1)} collective-permute-done((f32[4,2,8,2048]{3,2,1,0:T(8,128)S(1)}, f32[4,2,8,2048]{3,2,1,0:T(8,128)S(1)}, u32[]{:S(2)}, u32[]{:S(2)}) %collective-permute-start) | collective-permute-done | bytes 524320 | tf_op jit(solution)/shard_map/while/body/eval_jaxpr/ppermute | solution.py:27
  188.2 6.8 collective-permute-start
  195.0 27.6 %collective-permute-done = f32[4,2,8,2048]{3,2,1,0:T(8,128)S(1)} collective-permute-done((f32[4,2,8,2048]{3,2,1,0:T(8,128)S(1)}, f32[4,2,8,2048]{3,2,1,0:T(8,128)S(1)}, u32[]{:S(2)}, u32[]{:S(2)}) %collective-permute-start) | collective-permute-done | bytes 524320 | tf_op jit(solution)/shard_map/while/body/eval_jaxpr/ppermute | solution.py:27
  232.1 90.6 %collective-permute-done = f32[4,2,8,2048]{3,2,1,0:T(8,128)S(1)} collective-permute-done((f32[4,2,8,2048]{3,2,1,0:T(8,128)S(1)}, f32[4,2,8,2048]{3,2,1,0:T(8,128)S(1)}, u32[]{:S(2)}, u32[]{:S(2)}) %collective-permute-start) | collective-permute-done | bytes 524320 | tf_op jit(solution)/shard_map/while/body/eval_jaxpr/ppermute | solution.py:27
  330.2 8.4 collective-permute-start
  338.6 54.5 %collective-permute-done = f32[4,2,8,2048]{3,2,1,0:T(8,128)S(1)} collective-permute-done((f32[4,2,8,2048]{3,2,1,0:T(8,128)S(1)}, f32[4,2,8,2048]{3,2,1,0:T(8,128)S(1)}, u32[]{:S(2)}, u32[]{:S(2)}) %collective-permute-start) | collective-permute-done | bytes 524320 | tf_op jit(solution)/shard_map/while/body/eval_jaxpr/ppermute | solution.py:27
  402.6 14.2 %collective-permute-done = f32[4,2,8,2048]{3,2,1,0:T(8,128)S(1)} collective-permute-done((f32[4,2,8,2048]{3,2,1,0:T(8,128)S(1)}, f32[4,2,8,2048]{3,2,1,0:T(8,128)S(1)}, u32[]{:S(2)}, u32[]{:S(2)}) %collective-permute-start) | collective-permute-done | bytes 524320 | tf_op jit(solution)/shard_map/while/body/eval_jaxpr/ppermute | solution.py:27
  424.4 78.4 %collective-permute-start = (f32[4,2,8,2048]{3,2,1,0:T(8,128)S(1)}, f32[4,2,8,2048]{3,2,1,0:T(8,128)S(1)}, u32[]{:S(2)}, u32[]{:S(2)}) collective-permute-start(f32[4,2,8,2048]{3,2,1,0:T(8,128)S(1)} %pad_maximum_fusion.12), channel_id=1, source_target_pairs={{0,32},{32,64},{64,96},{96,128},{128,160},{160,192},{192,224},{224... | collective-permute-start | bytes 1572872 | tf_op jit(solution)/shard_map/while/body/eval_jaxpr/ppermute | solution.py:27
  502.8 10.5 %collective-permute-done = f32[4,2,8,2048]{3,2,1,0:T(8,128)S(1)} collective-permute-done((f32[4,2,8,2048]{3,2,1,0:T(8,128)S(1)}, f32[4,2,8,2048]{3,2,1,0:T(8,128)S(1)}, u32[]{:S(2)}, u32[]{:S(2)}) %collective-permute-start) | collective-permute-done | bytes 524320 | tf_op jit(solution)/shard_map/while/body/eval_jaxpr/ppermute | solution.py:27
  520.9 38.9 %collective-permute-start = (f32[4,2,8,2048]{3,2,1,0:T(8,128)S(1)}, f32[4,2,8,2048]{3,2,1,0:T(8,128)S(1)}, u32[]{:S(2)}, u32[]{:S(2)}) collective-permute-start(f32[4,2,8,2048]{3,2,1,0:T(8,128)S(1)} %pad_maximum_fusion.12), channel_id=1, source_target_pairs={{0,32},{32,64},{64,96},{96,128},{128,160},{160,192},{192,224},{224... | collective-permute-start | bytes 1572872 | tf_op jit(solution)/shard_map/while/body/eval_jaxpr/ppermute | solution.py:27
  559.8 9.2 collective-permute-done
  576.6 86.0 %collective-permute-start = (f32[4,2,8,2048]{3,2,1,0:T(8,128)S(1)}, f32[4,2,8,2048]{3,2,1,0:T(8,128)S(1)}, u32[]{:S(2)}, u32[]{:S(2)}) collective-permute-start(f32[4,2,8,2048]{3,2,1,0:T(8,128)S(1)} %pad_maximum_fusion.12), channel_id=1, source_target_pairs={{0,32},{32,64},{64,96},{96,128},{128,160},{160,192},{192,224},{224... | collective-permute-start | bytes 1572872 | tf_op jit(solution)/shard_map/while/body/eval_jaxpr/ppermute | solution.py:27
  662.6 70.1 %collective-permute-done = f32[4,2,8,2048]{3,2,1,0:T(8,128)S(1)} collective-permute-done((f32[4,2,8,2048]{3,2,1,0:T(8,128)S(1)}, f32[4,2,8,2048]{3,2,1,0:T(8,128)S(1)}, u32[]{:S(2)}, u32[]{:S(2)}) %collective-permute-start) | collective-permute-done | bytes 524320 | tf_op jit(solution)/shard_map/while/body/eval_jaxpr/ppermute | solution.py:27
  740.3 38.8 %collective-permute-start = (f32[4,2,8,2048]{3,2,1,0:T(8,128)S(1)}, f32[4,2,8,2048]{3,2,1,0:T(8,128)S(1)}, u32[]{:S(2)}, u32[]{:S(2)}) collective-permute-start(f32[4,2,8,2048]{3,2,1,0:T(8,128)S(1)} %pad_maximum_fusion.12), channel_id=1, source_target_pairs={{0,32},{32,64},{64,96},{96,128},{128,160},{160,192},{192,224},{224... | collective-permute-start | bytes 1572872 | tf_op jit(solution)/shard_map/while/body/eval_jaxpr/ppermute | solution.py:27
  779.2 52.8 %collective-permute-done = f32[4,2,8,2048]{3,2,1,0:T(8,128)S(1)} collective-permute-done((f32[4,2,8,2048]{3,2,1,0:T(8,128)S(1)}, f32[4,2,8,2048]{3,2,1,0:T(8,128)S(1)}, u32[]{:S(2)}, u32[]{:S(2)}) %collective-permute-start) | collective-permute-done | bytes 524320 | tf_op jit(solution)/shard_map/while/body/eval_jaxpr/ppermute | solution.py:27
  839.5 8.3 collective-permute-start
  847.8 27.7 %collective-permute-done = f32[4,2,8,2048]{3,2,1,0:T(8,128)S(1)} collective-permute-done((f32[4,2,8,2048]{3,2,1,0:T(8,128)S(1)}, f32[4,2,8,2048]{3,2,1,0:T(8,128)S(1)}, u32[]{:S(2)}, u32[]{:S(2)}) %collective-permute-start) | collective-permute-done | bytes 524320 | tf_op jit(solution)/shard_map/while/body/eval_jaxpr/ppermute | solution.py:27
  883.2 8.3 collective-permute-start
  891.5 7.7 collective-permute-done
  906.8 12.1 %collective-permute-start = (f32[4,2,8,2048]{3,2,1,0:T(8,128)S(1)}, f32[4,2,8,2048]{3,2,1,0:T(8,128)S(1)}, u32[]{:S(2)}, u32[]{:S(2)}) collective-permute-start(f32[4,2,8,2048]{3,2,1,0:T(8,128)S(1)} %pad_maximum_fusion.12), channel_id=1, source_target_pairs={{0,32},{32,64},{64,96},{96,128},{128,160},{160,192},{192,224},{224... | collective-permute-start | bytes 1572872 | tf_op jit(solution)/shard_map/while/body/eval_jaxpr/ppermute | solution.py:27
  918.9 12.8 %collective-permute-done = f32[4,2,8,2048]{3,2,1,0:T(8,128)S(1)} collective-permute-done((f32[4,2,8,2048]{3,2,1,0:T(8,128)S(1)}, f32[4,2,8,2048]{3,2,1,0:T(8,128)S(1)}, u32[]{:S(2)}, u32[]{:S(2)}) %collective-permute-start) | collective-permute-done | bytes 524320 | tf_op jit(solution)/shard_map/while/body/eval_jaxpr/ppermute | solution.py:27
  939.2 8.3 collective-permute-start
  947.5 20.1 %collective-permute-done = f32[4,2,8,2048]{3,2,1,0:T(8,128)S(1)} collective-permute-done((f32[4,2,8,2048]{3,2,1,0:T(8,128)S(1)}, f32[4,2,8,2048]{3,2,1,0:T(8,128)S(1)}, u32[]{:S(2)}, u32[]{:S(2)}) %collective-permute-start) | collective-permute-done | bytes 524320 | tf_op jit(solution)/shard_map/while/body/eval_jaxpr/ppermute | solution.py:27
  978.2 21.6 %collective-permute-done = f32[4,2,8,2048]{3,2,1,0:T(8,128)S(1)} collective-permute-done((f32[4,2,8,2048]{3,2,1,0:T(8,128)S(1)}, f32[4,2,8,2048]{3,2,1,0:T(8,128)S(1)}, u32[]{:S(2)}, u32[]{:S(2)}) %collective-permute-start) | collective-permute-done | bytes 524320 | tf_op jit(solution)/shard_map/while/body/eval_jaxpr/ppermute | solution.py:27
  1009.3 14.0 %collective-permute-done = f32[4,2,8,2048]{3,2,1,0:T(8,128)S(1)} collective-permute-done((f32[4,2,8,2048]{3,2,1,0:T(8,128)S(1)}, f32[4,2,8,2048]{3,2,1,0:T(8,128)S(1)}, u32[]{:S(2)}, u32[]{:S(2)}) %collective-permute-start) | collective-permute-done | bytes 524320 | tf_op jit(solution)/shard_map/while/body/eval_jaxpr/ppermute | solution.py:27
  (234 shorter events, 179.1 us)
Async XLA Ops:
  0.0 30.7 %copy-start = (f32[32,9]{0,1:T(8,128)S(1)}, f32[32,9]{0,1:T(8,128)}, u32[]{:S(2)}) copy-start(f32[32,9]{0,1:T(8,128)} %param.11) | copy-start | bytes 3460
  1.1 14.3 %collective-permute-start.1 = (f32[3,2,2048]{2,1,0:T(2,128)S(1)}, f32[3,2,2048]{2,1,0:T(2,128)S(1)}, u32[]{:S(2)}, u32[]{:S(2)}) collective-permute-start(f32[3,2,2048]{2,1,0:T(2,128)S(1)} %get-tuple-element.225), channel_id=1, source_target_pairs={{0,1},{1,2},{2,3},{3,4},{4,5},{5,6},{6,7},{7,8},{8,9},{9,10},{10,1... | collective-permute-start | bytes 147464 | tf_op jit(solution)/shard_map/ppermute | solution.py:16
  3.0 12.4 %collective-permute-start.2 = (f32[3,2,2048]{2,1,0:T(2,128)S(1)}, f32[3,2,2048]{2,1,0:T(2,128)S(1)}, u32[]{:S(2)}, u32[]{:S(2)}) collective-permute-start(f32[3,2,2048]{2,1,0:T(2,128)S(1)} %get-tuple-element.226), channel_id=1, source_target_pairs={{1,0},{2,1},{3,2},{4,3},{5,4},{6,5},{7,6},{8,7},{9,8},{10,9},{11,1... | collective-permute-start | bytes 147464 | tf_op jit(solution)/shard_map/ppermute | solution.py:19
  30.7 7.6 copy-start.5
  30.8 7.6 copy-start.6
  43.0 53.4 %copy-start.3 = (f32[64]{0:T(128)S(1)}, f32[64]{0:T(128)}, u32[]{:S(2)}) copy-start(f32[64]{0:T(128)} %iota_convert_fusion.1) | copy-start | bytes 772
  43.0 53.4 %copy-start.4 = (f32[2]{0:T(128)S(1)}, f32[2]{0:T(128)}, u32[]{:S(2)}) copy-start(f32[2]{0:T(128)} %add_convert_fusion) | copy-start | bytes 28
  43.0 53.9 %copy-start.2 = (f32[512]{0:T(512)S(1)}, f32[512]{0:T(512)}, u32[]{:S(2)}) copy-start(f32[512]{0:T(512)} %iota_convert_fusion) | copy-start | bytes 6148
  50.9 50.8 %collective-permute-start.3 = (f32[3,2,2048]{2,1,0:T(2,128)}, f32[3,2,2048]{2,1,0:T(2,128)}, u32[]{:S(2)}, u32[]{:S(2)}) collective-permute-start(f32[3,2,2048]{2,1,0:T(2,128)} %get-tuple-element.221), channel_id=1, source_target_pairs={{0,1},{1,2},{2,3},{3,4},{4,5},{5,6},{6,7},{7,8},{8,9},{9,10},{10,1... | collective-permute-start | bytes 147464 | tf_op jit(solution)/shard_map/ppermute | solution.py:16
  52.8 48.9 %collective-permute-start.4 = (f32[3,2,2048]{2,1,0:T(2,128)}, f32[3,2,2048]{2,1,0:T(2,128)}, u32[]{:S(2)}, u32[]{:S(2)}) collective-permute-start(f32[3,2,2048]{2,1,0:T(2,128)} %get-tuple-element.222), channel_id=1, source_target_pairs={{1,0},{2,1},{3,2},{4,3},{5,4},{6,5},{7,6},{8,7},{9,8},{10,9},{11,1... | collective-permute-start | bytes 147464 | tf_op jit(solution)/shard_map/ppermute | solution.py:19
  101.7 26.3 %copy-start.1 = (f32[4,2]{1,0:T(4,128)S(1)}, f32[4,2]{1,0:T(4,128)}, u32[]{:S(2)}) copy-start(f32[4,2]{1,0:T(4,128)} %constant.62.clone) | copy-start | bytes 100
  120.3 6.8 collective-permute-start.5
  122.2 5.1 collective-permute-start.6
  135.6 45.0 %collective-permute-start = (f32[4,2,8,2048]{3,2,1,0:T(8,128)S(1)}, f32[4,2,8,2048]{3,2,1,0:T(8,128)S(1)}, u32[]{:S(2)}, u32[]{:S(2)}) collective-permute-start(f32[4,2,8,2048]{3,2,1,0:T(8,128)S(1)} %pad_maximum_fusion.12), channel_id=1, source_target_pairs={{0,32},{32,64},{64,96},{96,128},{128,160},{160,192},{192,224},{224... | collective-permute-start | bytes 1572872 | tf_op jit(solution)/shard_map/while/body/eval_jaxpr/ppermute | solution.py:27
  188.2 34.4 %collective-permute-start = (f32[4,2,8,2048]{3,2,1,0:T(8,128)S(1)}, f32[4,2,8,2048]{3,2,1,0:T(8,128)S(1)}, u32[]{:S(2)}, u32[]{:S(2)}) collective-permute-start(f32[4,2,8,2048]{3,2,1,0:T(8,128)S(1)} %pad_maximum_fusion.12), channel_id=1, source_target_pairs={{0,32},{32,64},{64,96},{96,128},{128,160},{160,192},{192,224},{224... | collective-permute-start | bytes 1572872 | tf_op jit(solution)/shard_map/while/body/eval_jaxpr/ppermute | solution.py:27
  230.1 92.5 %collective-permute-start = (f32[4,2,8,2048]{3,2,1,0:T(8,128)S(1)}, f32[4,2,8,2048]{3,2,1,0:T(8,128)S(1)}, u32[]{:S(2)}, u32[]{:S(2)}) collective-permute-start(f32[4,2,8,2048]{3,2,1,0:T(8,128)S(1)} %pad_maximum_fusion.12), channel_id=1, source_target_pairs={{0,32},{32,64},{64,96},{96,128},{128,160},{160,192},{192,224},{224... | collective-permute-start | bytes 1572872 | tf_op jit(solution)/shard_map/while/body/eval_jaxpr/ppermute | solution.py:27
  330.2 62.8 %collective-permute-start = (f32[4,2,8,2048]{3,2,1,0:T(8,128)S(1)}, f32[4,2,8,2048]{3,2,1,0:T(8,128)S(1)}, u32[]{:S(2)}, u32[]{:S(2)}) collective-permute-start(f32[4,2,8,2048]{3,2,1,0:T(8,128)S(1)} %pad_maximum_fusion.12), channel_id=1, source_target_pairs={{0,32},{32,64},{64,96},{96,128},{128,160},{160,192},{192,224},{224... | collective-permute-start | bytes 1572872 | tf_op jit(solution)/shard_map/while/body/eval_jaxpr/ppermute | solution.py:27
  400.6 16.1 %collective-permute-start = (f32[4,2,8,2048]{3,2,1,0:T(8,128)S(1)}, f32[4,2,8,2048]{3,2,1,0:T(8,128)S(1)}, u32[]{:S(2)}, u32[]{:S(2)}) collective-permute-start(f32[4,2,8,2048]{3,2,1,0:T(8,128)S(1)} %pad_maximum_fusion.12), channel_id=1, source_target_pairs={{0,32},{32,64},{64,96},{96,128},{128,160},{160,192},{192,224},{224... | collective-permute-start | bytes 1572872 | tf_op jit(solution)/shard_map/while/body/eval_jaxpr/ppermute | solution.py:27
  424.4 89.0 %collective-permute-start = (f32[4,2,8,2048]{3,2,1,0:T(8,128)S(1)}, f32[4,2,8,2048]{3,2,1,0:T(8,128)S(1)}, u32[]{:S(2)}, u32[]{:S(2)}) collective-permute-start(f32[4,2,8,2048]{3,2,1,0:T(8,128)S(1)} %pad_maximum_fusion.12), channel_id=1, source_target_pairs={{0,32},{32,64},{64,96},{96,128},{128,160},{160,192},{192,224},{224... | collective-permute-start | bytes 1572872 | tf_op jit(solution)/shard_map/while/body/eval_jaxpr/ppermute | solution.py:27
  520.9 48.1 %collective-permute-start = (f32[4,2,8,2048]{3,2,1,0:T(8,128)S(1)}, f32[4,2,8,2048]{3,2,1,0:T(8,128)S(1)}, u32[]{:S(2)}, u32[]{:S(2)}) collective-permute-start(f32[4,2,8,2048]{3,2,1,0:T(8,128)S(1)} %pad_maximum_fusion.12), channel_id=1, source_target_pairs={{0,32},{32,64},{64,96},{96,128},{128,160},{160,192},{192,224},{224... | collective-permute-start | bytes 1572872 | tf_op jit(solution)/shard_map/while/body/eval_jaxpr/ppermute | solution.py:27
  576.6 156.1 %collective-permute-start = (f32[4,2,8,2048]{3,2,1,0:T(8,128)S(1)}, f32[4,2,8,2048]{3,2,1,0:T(8,128)S(1)}, u32[]{:S(2)}, u32[]{:S(2)}) collective-permute-start(f32[4,2,8,2048]{3,2,1,0:T(8,128)S(1)} %pad_maximum_fusion.12), channel_id=1, source_target_pairs={{0,32},{32,64},{64,96},{96,128},{128,160},{160,192},{192,224},{224... | collective-permute-start | bytes 1572872 | tf_op jit(solution)/shard_map/while/body/eval_jaxpr/ppermute | solution.py:27
  740.3 91.6 %collective-permute-start = (f32[4,2,8,2048]{3,2,1,0:T(8,128)S(1)}, f32[4,2,8,2048]{3,2,1,0:T(8,128)S(1)}, u32[]{:S(2)}, u32[]{:S(2)}) collective-permute-start(f32[4,2,8,2048]{3,2,1,0:T(8,128)S(1)} %pad_maximum_fusion.12), channel_id=1, source_target_pairs={{0,32},{32,64},{64,96},{96,128},{128,160},{160,192},{192,224},{224... | collective-permute-start | bytes 1572872 | tf_op jit(solution)/shard_map/while/body/eval_jaxpr/ppermute | solution.py:27
  839.5 36.1 %collective-permute-start = (f32[4,2,8,2048]{3,2,1,0:T(8,128)S(1)}, f32[4,2,8,2048]{3,2,1,0:T(8,128)S(1)}, u32[]{:S(2)}, u32[]{:S(2)}) collective-permute-start(f32[4,2,8,2048]{3,2,1,0:T(8,128)S(1)} %pad_maximum_fusion.12), channel_id=1, source_target_pairs={{0,32},{32,64},{64,96},{96,128},{128,160},{160,192},{192,224},{224... | collective-permute-start | bytes 1572872 | tf_op jit(solution)/shard_map/while/body/eval_jaxpr/ppermute | solution.py:27
  883.2 16.0 %collective-permute-start = (f32[4,2,8,2048]{3,2,1,0:T(8,128)S(1)}, f32[4,2,8,2048]{3,2,1,0:T(8,128)S(1)}, u32[]{:S(2)}, u32[]{:S(2)}) collective-permute-start(f32[4,2,8,2048]{3,2,1,0:T(8,128)S(1)} %pad_maximum_fusion.12), channel_id=1, source_target_pairs={{0,32},{32,64},{64,96},{96,128},{128,160},{160,192},{192,224},{224... | collective-permute-start | bytes 1572872 | tf_op jit(solution)/shard_map/while/body/eval_jaxpr/ppermute | solution.py:27
  906.8 24.9 %collective-permute-start = (f32[4,2,8,2048]{3,2,1,0:T(8,128)S(1)}, f32[4,2,8,2048]{3,2,1,0:T(8,128)S(1)}, u32[]{:S(2)}, u32[]{:S(2)}) collective-permute-start(f32[4,2,8,2048]{3,2,1,0:T(8,128)S(1)} %pad_maximum_fusion.12), channel_id=1, source_target_pairs={{0,32},{32,64},{64,96},{96,128},{128,160},{160,192},{192,224},{224... | collective-permute-start | bytes 1572872 | tf_op jit(solution)/shard_map/while/body/eval_jaxpr/ppermute | solution.py:27
  939.2 28.4 %collective-permute-start = (f32[4,2,8,2048]{3,2,1,0:T(8,128)S(1)}, f32[4,2,8,2048]{3,2,1,0:T(8,128)S(1)}, u32[]{:S(2)}, u32[]{:S(2)}) collective-permute-start(f32[4,2,8,2048]{3,2,1,0:T(8,128)S(1)} %pad_maximum_fusion.12), channel_id=1, source_target_pairs={{0,32},{32,64},{64,96},{96,128},{128,160},{160,192},{192,224},{224... | collective-permute-start | bytes 1572872 | tf_op jit(solution)/shard_map/while/body/eval_jaxpr/ppermute | solution.py:27
  975.2 24.6 %collective-permute-start = (f32[4,2,8,2048]{3,2,1,0:T(8,128)S(1)}, f32[4,2,8,2048]{3,2,1,0:T(8,128)S(1)}, u32[]{:S(2)}, u32[]{:S(2)}) collective-permute-start(f32[4,2,8,2048]{3,2,1,0:T(8,128)S(1)} %pad_maximum_fusion.12), channel_id=1, source_target_pairs={{0,32},{32,64},{64,96},{96,128},{128,160},{160,192},{192,224},{224... | collective-permute-start | bytes 1572872 | tf_op jit(solution)/shard_map/while/body/eval_jaxpr/ppermute | solution.py:27
  1007.4 15.9 %collective-permute-start = (f32[4,2,8,2048]{3,2,1,0:T(8,128)S(1)}, f32[4,2,8,2048]{3,2,1,0:T(8,128)S(1)}, u32[]{:S(2)}, u32[]{:S(2)}) collective-permute-start(f32[4,2,8,2048]{3,2,1,0:T(8,128)S(1)} %pad_maximum_fusion.12), channel_id=1, source_target_pairs={{0,32},{32,64},{64,96},{96,128},{128,160},{160,192},{192,224},{224... | collective-permute-start | bytes 1572872 | tf_op jit(solution)/shard_map/while/body/eval_jaxpr/ppermute | solution.py:27
where the time goes:
time: 1030 us
  waiting for transfers between devices  469 us (46%)
  starting transfers between devices  328 us (32%)
  other arithmetic  138 us (13%)
  local copies, waits for them, and re-layouts  43.6 us (4%)
  blocking collectives  36.7 us (4%)
  matrix products  12.7 us (1%)
    ppermute x15, waiting for transfers between devices, from_behind(): return lax.ppermute(value, axis, pairs)  469 us
    ppermute x15, starting transfers between devices, from_behind(): return lax.ppermute(value, axis, pairs)  312 us
    sub x48, other arithmetic, lens_step(): (1.0 - mixing) * previous + mixing * current - bending * bent_rows  105 us
    all_gather x1, blocking collectives, body(): received = lax.all_gather(coarse, 'tile', axis=1, tiled=True)  36.7 us
  transfers between devices with their start and end apart: 21, of which 16 were waited for; matrix products, arithmetic and copies ran while one was open for 2% of the time, Pallas kernels for 0%

commit v1 on v0

--- a/solution.py
+++ b/solution.py
@@ -130,7 +130,9 @@
     short_part = short_rows(convergence_wide, short_kernel)
     row_global = tile_index * coarse_here + 0 + jnp.arange(coarse_here, dtype=jnp.int32)
     coarse = convergence.reshape(plane_count, coarse_here, 4, coarse_cols, 4).mean(axis=(2, 4))
-    received = lax.all_gather(coarse, "tile", axis=1, tiled=True)
+    received = jnp.concatenate(
+        lax.all_to_all(jnp.stack([coarse] * lax.axis_size("tile")), "tile", 0, 0), axis=1
+    )
     span_cols = received.shape[1]
     kernel_block = coarse_kernel(row_global, jnp.arange(span_cols, dtype=jnp.int32), row_scale)
     summed = jnp.einsum("ik,pkx->pix", kernel_block, received, precision=highest)

time: 1030 us -> 991 us (0.962)
  the two profiles are of different devices: /device:TPU:108 before, /device:TPU:106 now
where the time goes in v1:
time: 991 us; the launch traced here: 988 us
  waiting for transfers between devices  613 us (62%)
  starting transfers between devices  187 us (19%)
  other arithmetic  130 us (13%)
  local copies, waits for them, and re-layouts  42.6 us (4%)
  matrix products  12.6 us (1%)
    ppermute x15, waiting for transfers between devices, from_behind(): return lax.ppermute(value, axis, pairs)  611 us
    ppermute x15, starting transfers between devices, from_behind(): return lax.ppermute(value, axis, pairs)  160 us
    sub x48, other arithmetic, lens_step(): (1.0 - mixing) * previous + mixing * current - bending * bent_rows  102 us
  transfers between devices with their start and end apart: 22, of which 19 were waited for; matrix products, arithmetic and copies ran while one was open for 1% of the time, Pallas kernels for 0%

profile of v1, /device:TPU:106, one launch (start us, length us, event | category | flops | bytes accessed | tf_op | source)
XLA Modules:
  0.0 988.4 jit_solution(5103834122238602432)
XLA Ops:
  17.2 6.6 stack.68
  23.8 7.6 fusion.60
  35.4 7.9 reshape.73
  47.4 9.6 all-to-all-start
  73.4 16.4 %fusion.32 = f32[3,8,2048]{2,1,0:T(8,128)S(1)} fusion(f32[3,8,2048]{2,1,0:T(8,128)S(1)} %copy.171, f32[3,8,2048]{2,1,0:T(8,128)S(1)} %bitcast.139, f32[3,2,2048]{2,1,0:T(2,128)S(1)} %collective-permute-done.4, f32[3,2,2048]{2,1,0:T(2,128)S(1)} %collective-permute-done.3, f32[3,12,2052]{2,1,0:T(8,128)S(1)} %select_maximum_fusion.2, f32[]{:T(128)} %bitcast.37, ...), kind=kLoop, calls=%fused_computation.73 | loop fusion | flops 2654208 | bytes 4620388 | tf_op jit(solution)/shard_map/add | solution.py:139
  99.6 881.2 %while.13 = (s32[]{:T(128)}, f32[4,2,8,2048]{3,2,1,0:T(8,128)S(1)}, pred[]{:T(512)}, f32[]{:T(128)}, f32[3]{0:T(128)S(1)}, /*index=5*/f32[]{:T(128)}, f32[3]{0:T...) while((s32[]{:T(128)}, f32[4,2,8,2048]{3,2,1,0:T(8,128)S(1)}, ...), condition=%wide.region_2.3_spmd.clone, body=%wide.region_1.2_spmd.sunk.clone.sunk | while | flops 2818050 | bytes 11469090 | solution.py:168
  106.9 9.1 collective-permute-start
  116.0 47.5 %collective-permute-done = f32[4,2,8,2048]{3,2,1,0:T(8,128)S(1)} collective-permute-done((f32[4,2,8,2048]{3,2,1,0:T(8,128)S(1)}, f32[4,2,8,2048]{3,2,1,0:T(8,128)S(1)}, u32[]{:S(2)}, u32[]{:S(2)}) %collective-permute-start) | collective-permute-done | bytes 524320 | tf_op jit(solution)/shard_map/while/body/eval_jaxpr/ppermute | solution.py:27
  170.9 6.4 collective-permute-start
  177.3 36.3 %collective-permute-done = f32[4,2,8,2048]{3,2,1,0:T(8,128)S(1)} collective-permute-done((f32[4,2,8,2048]{3,2,1,0:T(8,128)S(1)}, f32[4,2,8,2048]{3,2,1,0:T(8,128)S(1)}, u32[]{:S(2)}, u32[]{:S(2)}) %collective-permute-start) | collective-permute-done | bytes 524320 | tf_op jit(solution)/shard_map/while/body/eval_jaxpr/ppermute | solution.py:27
  223.3 67.9 %collective-permute-done = f32[4,2,8,2048]{3,2,1,0:T(8,128)S(1)} collective-permute-done((f32[4,2,8,2048]{3,2,1,0:T(8,128)S(1)}, f32[4,2,8,2048]{3,2,1,0:T(8,128)S(1)}, u32[]{:S(2)}, u32[]{:S(2)}) %collective-permute-start) | collective-permute-done | bytes 524320 | tf_op jit(solution)/shard_map/while/body/eval_jaxpr/ppermute | solution.py:27
  298.5 8.3 collective-permute-start
  306.8 89.2 %collective-permute-done = f32[4,2,8,2048]{3,2,1,0:T(8,128)S(1)} collective-permute-done((f32[4,2,8,2048]{3,2,1,0:T(8,128)S(1)}, f32[4,2,8,2048]{3,2,1,0:T(8,128)S(1)}, u32[]{:S(2)}, u32[]{:S(2)}) %collective-permute-start) | collective-permute-done | bytes 524320 | tf_op jit(solution)/shard_map/while/body/eval_jaxpr/ppermute | solution.py:27
  405.3 40.3 %collective-permute-done = f32[4,2,8,2048]{3,2,1,0:T(8,128)S(1)} collective-permute-done((f32[4,2,8,2048]{3,2,1,0:T(8,128)S(1)}, f32[4,2,8,2048]{3,2,1,0:T(8,128)S(1)}, u32[]{:S(2)}, u32[]{:S(2)}) %collective-permute-start) | collective-permute-done | bytes 524320 | tf_op jit(solution)/shard_map/while/body/eval_jaxpr/ppermute | solution.py:27
  452.9 8.3 collective-permute-start
  461.2 56.1 %collective-permute-done = f32[4,2,8,2048]{3,2,1,0:T(8,128)S(1)} collective-permute-done((f32[4,2,8,2048]{3,2,1,0:T(8,128)S(1)}, f32[4,2,8,2048]{3,2,1,0:T(8,128)S(1)}, u32[]{:S(2)}, u32[]{:S(2)}) %collective-permute-start) | collective-permute-done | bytes 524320 | tf_op jit(solution)/shard_map/while/body/eval_jaxpr/ppermute | solution.py:27
  526.6 46.7 %collective-permute-done = f32[4,2,8,2048]{3,2,1,0:T(8,128)S(1)} collective-permute-done((f32[4,2,8,2048]{3,2,1,0:T(8,128)S(1)}, f32[4,2,8,2048]{3,2,1,0:T(8,128)S(1)}, u32[]{:S(2)}, u32[]{:S(2)}) %collective-permute-start) | collective-permute-done | bytes 524320 | tf_op jit(solution)/shard_map/while/body/eval_jaxpr/ppermute | solution.py:27
  580.7 6.9 collective-permute-start
  587.6 30.3 %collective-permute-done = f32[4,2,8,2048]{3,2,1,0:T(8,128)S(1)} collective-permute-done((f32[4,2,8,2048]{3,2,1,0:T(8,128)S(1)}, f32[4,2,8,2048]{3,2,1,0:T(8,128)S(1)}, u32[]{:S(2)}, u32[]{:S(2)}) %collective-permute-start) | collective-permute-done | bytes 524320 | tf_op jit(solution)/shard_map/while/body/eval_jaxpr/ppermute | solution.py:27
  625.3 65.3 %collective-permute-start = (f32[4,2,8,2048]{3,2,1,0:T(8,128)S(1)}, f32[4,2,8,2048]{3,2,1,0:T(8,128)S(1)}, u32[]{:S(2)}, u32[]{:S(2)}) collective-permute-start(f32[4,2,8,2048]{3,2,1,0:T(8,128)S(1)} %pad_maximum_fusion.12), channel_id=1, source_target_pairs={{0,32},{32,64},{64,96},{96,128},{128,160},{160,192},{192,224},{224... | collective-permute-start | bytes 1572872 | tf_op jit(solution)/shard_map/while/body/eval_jaxpr/ppermute | solution.py:27
  690.6 20.3 %collective-permute-done = f32[4,2,8,2048]{3,2,1,0:T(8,128)S(1)} collective-permute-done((f32[4,2,8,2048]{3,2,1,0:T(8,128)S(1)}, f32[4,2,8,2048]{3,2,1,0:T(8,128)S(1)}, u32[]{:S(2)}, u32[]{:S(2)}) %collective-permute-start) | collective-permute-done | bytes 524320 | tf_op jit(solution)/shard_map/while/body/eval_jaxpr/ppermute | solution.py:27
  718.2 21.8 %collective-permute-start = (f32[4,2,8,2048]{3,2,1,0:T(8,128)S(1)}, f32[4,2,8,2048]{3,2,1,0:T(8,128)S(1)}, u32[]{:S(2)}, u32[]{:S(2)}) collective-permute-start(f32[4,2,8,2048]{3,2,1,0:T(8,128)S(1)} %pad_maximum_fusion.12), channel_id=1, source_target_pairs={{0,32},{32,64},{64,96},{96,128},{128,160},{160,192},{192,224},{224... | collective-permute-start | bytes 1572872 | tf_op jit(solution)/shard_map/while/body/eval_jaxpr/ppermute | solution.py:27
  740.1 85.0 %collective-permute-done = f32[4,2,8,2048]{3,2,1,0:T(8,128)S(1)} collective-permute-done((f32[4,2,8,2048]{3,2,1,0:T(8,128)S(1)}, f32[4,2,8,2048]{3,2,1,0:T(8,128)S(1)}, u32[]{:S(2)}, u32[]{:S(2)}) %collective-permute-start) | collective-permute-done | bytes 524320 | tf_op jit(solution)/shard_map/while/body/eval_jaxpr/ppermute | solution.py:27
  834.3 29.3 %collective-permute-done = f32[4,2,8,2048]{3,2,1,0:T(8,128)S(1)} collective-permute-done((f32[4,2,8,2048]{3,2,1,0:T(8,128)S(1)}, f32[4,2,8,2048]{3,2,1,0:T(8,128)S(1)}, u32[]{:S(2)}, u32[]{:S(2)}) %collective-permute-start) | collective-permute-done | bytes 524320 | tf_op jit(solution)/shard_map/while/body/eval_jaxpr/ppermute | solution.py:27
  871.0 8.3 collective-permute-start
  879.3 23.4 %collective-permute-done = f32[4,2,8,2048]{3,2,1,0:T(8,128)S(1)} collective-permute-done((f32[4,2,8,2048]{3,2,1,0:T(8,128)S(1)}, f32[4,2,8,2048]{3,2,1,0:T(8,128)S(1)}, u32[]{:S(2)}, u32[]{:S(2)}) %collective-permute-start) | collective-permute-done | bytes 524320 | tf_op jit(solution)/shard_map/while/body/eval_jaxpr/ppermute | solution.py:27
  910.0 5.9 collective-permute-start
  915.9 13.7 %collective-permute-done = f32[4,2,8,2048]{3,2,1,0:T(8,128)S(1)} collective-permute-done((f32[4,2,8,2048]{3,2,1,0:T(8,128)S(1)}, f32[4,2,8,2048]{3,2,1,0:T(8,128)S(1)}, u32[]{:S(2)}, u32[]{:S(2)}) %collective-permute-start) | collective-permute-done | bytes 524320 | tf_op jit(solution)/shard_map/while/body/eval_jaxpr/ppermute | solution.py:27
  936.9 5.8 collective-permute-start
  942.7 12.9 %collective-permute-done = f32[4,2,8,2048]{3,2,1,0:T(8,128)S(1)} collective-permute-done((f32[4,2,8,2048]{3,2,1,0:T(8,128)S(1)}, f32[4,2,8,2048]{3,2,1,0:T(8,128)S(1)}, u32[]{:S(2)}, u32[]{:S(2)}) %collective-permute-start) | collective-permute-done | bytes 524320 | tf_op jit(solution)/shard_map/while/body/eval_jaxpr/ppermute | solution.py:27
  963.0 5.8 collective-permute-start
  968.8 11.9 %collective-permute-done = f32[4,2,8,2048]{3,2,1,0:T(8,128)S(1)} collective-permute-done((f32[4,2,8,2048]{3,2,1,0:T(8,128)S(1)}, f32[4,2,8,2048]{3,2,1,0:T(8,128)S(1)}, u32[]{:S(2)}, u32[]{:S(2)}) %collective-permute-start) | collective-permute-done | bytes 524320 | tf_op jit(solution)/shard_map/while/body/eval_jaxpr/ppermute | solution.py:27
  (235 shorter events, 174.4 us)
Async XLA Ops:
  0.0 23.8 %copy-start = (f32[32,9]{0,1:T(8,128)S(1)}, f32[32,9]{0,1:T(8,128)}, u32[]{:S(2)}) copy-start(f32[32,9]{0,1:T(8,128)} %param.11) | copy-start | bytes 3460
  1.1 7.4 collective-permute-start.1
  3.0 5.5 collective-permute-start.2
  23.8 7.6 copy-start.4
  23.8 7.6 copy-start.5
  35.4 21.7 %copy-start.3 = (s32[48]{0:T(128)S(1)}, s32[48]{0:T(128)}, u32[]{:S(2)}) copy-start(s32[48]{0:T(128)} %param.10) | copy-start | bytes 580
  35.4 22.5 %copy-start.2 = (f32[5,5]{1,0:T(8,128)S(1)}, f32[5,5]{1,0:T(8,128)}, u32[]{:S(2)}) copy-start(f32[5,5]{1,0:T(8,128)} %param.14) | copy-start | bytes 304
  47.4 19.7 %all-to-all-start = ((f32[32,3,2,512]{3,2,1,0:T(2,128)}), f32[32,3,2,512]{3,2,1,0:T(2,128)S(1)}, u32[]{:S(2)}, u32[]{:S(2)}) async-start(f32[32,3,2,512]{3,2,1,0:T(2,128)} %stack.69), calls=%async_computation | async-start | bytes 786432 | tf_op jit(solution)/shard_map/all_to_all | solution.py:134
  59.3 5.8 collective-permute-start.3
  61.4 5.2 collective-permute-start.4
  71.1 28.5 %copy-start.1 = (f32[4,2]{1,0:T(4,128)S(1)}, f32[4,2]{1,0:T(4,128)}, u32[]{:S(2)}) copy-start(f32[4,2]{1,0:T(4,128)} %constant.62.clone) | copy-start | bytes 100
  89.8 8.4 collective-permute-start.5
  93.7 5.1 collective-permute-start.6
  106.9 56.6 %collective-permute-start = (f32[4,2,8,2048]{3,2,1,0:T(8,128)S(1)}, f32[4,2,8,2048]{3,2,1,0:T(8,128)S(1)}, u32[]{:S(2)}, u32[]{:S(2)}) collective-permute-start(f32[4,2,8,2048]{3,2,1,0:T(8,128)S(1)} %pad_maximum_fusion.12), channel_id=1, source_target_pairs={{0,32},{32,64},{64,96},{96,128},{128,160},{160,192},{192,224},{224... | collective-permute-start | bytes 1572872 | tf_op jit(solution)/shard_map/while/body/eval_jaxpr/ppermute | solution.py:27
  170.9 42.8 %collective-permute-start = (f32[4,2,8,2048]{3,2,1,0:T(8,128)S(1)}, f32[4,2,8,2048]{3,2,1,0:T(8,128)S(1)}, u32[]{:S(2)}, u32[]{:S(2)}) collective-permute-start(f32[4,2,8,2048]{3,2,1,0:T(8,128)S(1)} %pad_maximum_fusion.12), channel_id=1, source_target_pairs={{0,32},{32,64},{64,96},{96,128},{128,160},{160,192},{192,224},{224... | collective-permute-start | bytes 1572872 | tf_op jit(solution)/shard_map/while/body/eval_jaxpr/ppermute | solution.py:27
  221.0 70.2 %collective-permute-start = (f32[4,2,8,2048]{3,2,1,0:T(8,128)S(1)}, f32[4,2,8,2048]{3,2,1,0:T(8,128)S(1)}, u32[]{:S(2)}, u32[]{:S(2)}) collective-permute-start(f32[4,2,8,2048]{3,2,1,0:T(8,128)S(1)} %pad_maximum_fusion.12), channel_id=1, source_target_pairs={{0,32},{32,64},{64,96},{96,128},{128,160},{160,192},{192,224},{224... | collective-permute-start | bytes 1572872 | tf_op jit(solution)/shard_map/while/body/eval_jaxpr/ppermute | solution.py:27
  298.5 97.5 %collective-permute-start = (f32[4,2,8,2048]{3,2,1,0:T(8,128)S(1)}, f32[4,2,8,2048]{3,2,1,0:T(8,128)S(1)}, u32[]{:S(2)}, u32[]{:S(2)}) collective-permute-start(f32[4,2,8,2048]{3,2,1,0:T(8,128)S(1)} %pad_maximum_fusion.12), channel_id=1, source_target_pairs={{0,32},{32,64},{64,96},{96,128},{128,160},{160,192},{192,224},{224... | collective-permute-start | bytes 1572872 | tf_op jit(solution)/shard_map/while/body/eval_jaxpr/ppermute | solution.py:27
  403.4 42.2 %collective-permute-start = (f32[4,2,8,2048]{3,2,1,0:T(8,128)S(1)}, f32[4,2,8,2048]{3,2,1,0:T(8,128)S(1)}, u32[]{:S(2)}, u32[]{:S(2)}) collective-permute-start(f32[4,2,8,2048]{3,2,1,0:T(8,128)S(1)} %pad_maximum_fusion.12), channel_id=1, source_target_pairs={{0,32},{32,64},{64,96},{96,128},{128,160},{160,192},{192,224},{224... | collective-permute-start | bytes 1572872 | tf_op jit(solution)/shard_map/while/body/eval_jaxpr/ppermute | solution.py:27
  452.9 64.4 %collective-permute-start = (f32[4,2,8,2048]{3,2,1,0:T(8,128)S(1)}, f32[4,2,8,2048]{3,2,1,0:T(8,128)S(1)}, u32[]{:S(2)}, u32[]{:S(2)}) collective-permute-start(f32[4,2,8,2048]{3,2,1,0:T(8,128)S(1)} %pad_maximum_fusion.12), channel_id=1, source_target_pairs={{0,32},{32,64},{64,96},{96,128},{128,160},{160,192},{192,224},{224... | collective-permute-start | bytes 1572872 | tf_op jit(solution)/shard_map/while/body/eval_jaxpr/ppermute | solution.py:27
  524.7 48.6 %collective-permute-start = (f32[4,2,8,2048]{3,2,1,0:T(8,128)S(1)}, f32[4,2,8,2048]{3,2,1,0:T(8,128)S(1)}, u32[]{:S(2)}, u32[]{:S(2)}) collective-permute-start(f32[4,2,8,2048]{3,2,1,0:T(8,128)S(1)} %pad_maximum_fusion.12), channel_id=1, source_target_pairs={{0,32},{32,64},{64,96},{96,128},{128,160},{160,192},{192,224},{224... | collective-permute-start | bytes 1572872 | tf_op jit(solution)/shard_map/while/body/eval_jaxpr/ppermute | solution.py:27
  580.7 37.2 %collective-permute-start = (f32[4,2,8,2048]{3,2,1,0:T(8,128)S(1)}, f32[4,2,8,2048]{3,2,1,0:T(8,128)S(1)}, u32[]{:S(2)}, u32[]{:S(2)}) collective-permute-start(f32[4,2,8,2048]{3,2,1,0:T(8,128)S(1)} %pad_maximum_fusion.12), channel_id=1, source_target_pairs={{0,32},{32,64},{64,96},{96,128},{128,160},{160,192},{192,224},{224... | collective-permute-start | bytes 1572872 | tf_op jit(solution)/shard_map/while/body/eval_jaxpr/ppermute | solution.py:27
  625.3 85.6 %collective-permute-start = (f32[4,2,8,2048]{3,2,1,0:T(8,128)S(1)}, f32[4,2,8,2048]{3,2,1,0:T(8,128)S(1)}, u32[]{:S(2)}, u32[]{:S(2)}) collective-permute-start(f32[4,2,8,2048]{3,2,1,0:T(8,128)S(1)} %pad_maximum_fusion.12), channel_id=1, source_target_pairs={{0,32},{32,64},{64,96},{96,128},{128,160},{160,192},{192,224},{224... | collective-permute-start | bytes 1572872 | tf_op jit(solution)/shard_map/while/body/eval_jaxpr/ppermute | solution.py:27
  718.2 106.8 %collective-permute-start = (f32[4,2,8,2048]{3,2,1,0:T(8,128)S(1)}, f32[4,2,8,2048]{3,2,1,0:T(8,128)S(1)}, u32[]{:S(2)}, u32[]{:S(2)}) collective-permute-start(f32[4,2,8,2048]{3,2,1,0:T(8,128)S(1)} %pad_maximum_fusion.12), channel_id=1, source_target_pairs={{0,32},{32,64},{64,96},{96,128},{128,160},{160,192},{192,224},{224... | collective-permute-start | bytes 1572872 | tf_op jit(solution)/shard_map/while/body/eval_jaxpr/ppermute | solution.py:27
  832.4 31.3 %collective-permute-start = (f32[4,2,8,2048]{3,2,1,0:T(8,128)S(1)}, f32[4,2,8,2048]{3,2,1,0:T(8,128)S(1)}, u32[]{:S(2)}, u32[]{:S(2)}) collective-permute-start(f32[4,2,8,2048]{3,2,1,0:T(8,128)S(1)} %pad_maximum_fusion.12), channel_id=1, source_target_pairs={{0,32},{32,64},{64,96},{96,128},{128,160},{160,192},{192,224},{224... | collective-permute-start | bytes 1572872 | tf_op jit(solution)/shard_map/while/body/eval_jaxpr/ppermute | solution.py:27
  871.0 31.6 %collective-permute-start = (f32[4,2,8,2048]{3,2,1,0:T(8,128)S(1)}, f32[4,2,8,2048]{3,2,1,0:T(8,128)S(1)}, u32[]{:S(2)}, u32[]{:S(2)}) collective-permute-start(f32[4,2,8,2048]{3,2,1,0:T(8,128)S(1)} %pad_maximum_fusion.12), channel_id=1, source_target_pairs={{0,32},{32,64},{64,96},{96,128},{128,160},{160,192},{192,224},{224... | collective-permute-start | bytes 1572872 | tf_op jit(solution)/shard_map/while/body/eval_jaxpr/ppermute | solution.py:27
  910.0 19.6 %collective-permute-start = (f32[4,2,8,2048]{3,2,1,0:T(8,128)S(1)}, f32[4,2,8,2048]{3,2,1,0:T(8,128)S(1)}, u32[]{:S(2)}, u32[]{:S(2)}) collective-permute-start(f32[4,2,8,2048]{3,2,1,0:T(8,128)S(1)} %pad_maximum_fusion.12), channel_id=1, source_target_pairs={{0,32},{32,64},{64,96},{96,128},{128,160},{160,192},{192,224},{224... | collective-permute-start | bytes 1572872 | tf_op jit(solution)/shard_map/while/body/eval_jaxpr/ppermute | solution.py:27
  936.9 18.7 %collective-permute-start = (f32[4,2,8,2048]{3,2,1,0:T(8,128)S(1)}, f32[4,2,8,2048]{3,2,1,0:T(8,128)S(1)}, u32[]{:S(2)}, u32[]{:S(2)}) collective-permute-start(f32[4,2,8,2048]{3,2,1,0:T(8,128)S(1)} %pad_maximum_fusion.12), channel_id=1, source_target_pairs={{0,32},{32,64},{64,96},{96,128},{128,160},{160,192},{192,224},{224... | collective-permute-start | bytes 1572872 | tf_op jit(solution)/shard_map/while/body/eval_jaxpr/ppermute | solution.py:27
  963.0 17.7 %collective-permute-start = (f32[4,2,8,2048]{3,2,1,0:T(8,128)S(1)}, f32[4,2,8,2048]{3,2,1,0:T(8,128)S(1)}, u32[]{:S(2)}, u32[]{:S(2)}) collective-permute-start(f32[4,2,8,2048]{3,2,1,0:T(8,128)S(1)} %pad_maximum_fusion.12), channel_id=1, source_target_pairs={{0,32},{32,64},{64,96},{96,128},{128,160},{160,192},{192,224},{224... | collective-permute-start | bytes 1572872 | tf_op jit(solution)/shard_map/while/body/eval_jaxpr/ppermute | solution.py:27
